TPU v7x, 256 devices: a whole 4x4x8 slice. The times are simulated.
256 devices in a mesh: row: 32 (over y, x, z_hi), col: 8 (over z_lo, core).
Axes of the slice: x: 4, y: 4, z: 8 (z_hi: 2, z_lo: 4; z = z_hi * 4 + z_lo), core: 2. Of those that a mesh axis runs over, the one named last changes fastest.
Arguments:
- alignment: bfloat16 [64, 1536, 256], P('row', 'col'), may hold values from -6 to 6
- pair_act: bfloat16 [1536, 1536, 128], P('row', 'col'), may hold values from -600 to 600
- targets: int32 [1536, 1536], P('row', 'col'), may hold values from 0 to 63, as said below
- crop_mask: int32 [1536], replicated, may hold values 0 or 1
- projection_weight: bfloat16 [256, 64], replicated, may hold values from -0.375 to 0.375
- w_outer: bfloat16 [1024, 128], replicated, may hold values from -1.5 to 1.5
- w_expand: bfloat16 [128, 512], replicated, may hold values from -0.5 to 0.5
- w_shrink: bfloat16 [512, 128], replicated, may hold values from -0.25 to 0.25
- w_bins: bfloat16 [128, 64], replicated, may hold values from -1.8 to 1.8
Outputs:
- pair_grad: bfloat16 [1536, 1536, 128], P('row', 'col')
Inputs may be any that keep to these rules, and one draw needn't show every extreme that they name: targets[i, j] equals targets[j, i].
All inputs are finite; a program needn't handle non-finite values.
Results may differ from a plain program's by a relative error of at most 0.02.
The roundings to bfloat16 on the way count: a program that leaves them out, or rounds other values in their place, can miss the bound.
Values may be sent and summed in bfloat16 or wider, within the bound.
A program may use at most 128 MiB of HBM per device.

v0:
```python
import jax
import jax.numpy as jnp
from jax import lax
from jax.sharding import PartitionSpec as P

FACTOR_CHANNELS = 32
BINS = 64
SEQUENCE_COUNT = 64
epsilon = 1e-05


def from_root(shard, axis, root):
    mine = lax.axis_index(axis) == root
    return lax.psum(jnp.where(mine, shard, jnp.zeros_like(shard)), axis)


def layer_normalize(values):
    average = jnp.mean(values, axis=-1, keepdims=True)
    centred = values - average
    inverse_deviation = lax.rsqrt(jnp.mean(centred * centred, axis=-1, keepdims=True) + epsilon)
    return (centred * inverse_deviation, inverse_deviation)


def norm_project(shard_rows, projection_weight):
    normed = layer_normalize(shard_rows.astype(jnp.float32))[0].astype(jnp.bfloat16)
    factor = jnp.dot(normed, projection_weight, preferred_element_type=jnp.float32).astype(
        jnp.bfloat16
    )
    return factor.reshape(shard_rows.shape[0], -1)


def mirrored(tile_rows, rows_dev, n_row, n_col):
    ratio = n_row // n_col
    group_rows = tile_rows.shape[0] // n_col
    sectioned = tile_rows.reshape(n_col, group_rows, ratio, rows_dev * BINS).transpose(0, 2, 1, 3)
    first_hop = lax.all_to_all(sectioned, "col", split_axis=0, concat_axis=0, tiled=True)
    regrouped = first_hop.reshape(n_row, 1, group_rows, rows_dev * BINS)
    arrived = lax.all_to_all(
        lax.all_to_all(regrouped, "row", split_axis=0, concat_axis=1, tiled=True),
        "col",
        split_axis=1,
        concat_axis=0,
        tiled=True,
    )
    return arrived.reshape(n_col, ratio, group_rows, rows_dev, BINS).transpose(3, 1, 0, 2, 4)


def per_device(
    alignment, pair_act, targets, crop_mask, projection_weight, w_outer, w_expand, w_shrink, w_bins
):
    rows_dev, cols_dev, channels = pair_act.shape
    n_row = lax.axis_size("row")
    n_col = lax.axis_size("col")
    ratio = n_row // n_col
    row_index = lax.axis_index("row")
    col_index = lax.axis_index("col")
    factors = norm_project(lax.all_gather(alignment, "row", axis=0, tiled=True), projection_weight)
    factors = factors.reshape(SEQUENCE_COUNT, cols_dev, 2 * FACTOR_CHANNELS)
    right_side = factors[:, :, FACTOR_CHANNELS:]
    own_left = lax.dynamic_slice_in_dim(
        factors[:, :, :FACTOR_CHANNELS], row_index % ratio * rows_dev, rows_dev, 1
    )
    left_side = from_root(
        own_left.reshape(SEQUENCE_COUNT, rows_dev * FACTOR_CHANNELS), "col", row_index // ratio
    )
    left_side = left_side.reshape(SEQUENCE_COUNT, rows_dev, FACTOR_CHANNELS)
    block_rows = 8
    blocks = rows_dev // block_rows
    pair_blocks = pair_act.reshape(blocks, block_rows, cols_dev, channels)
    left_blocks = left_side.reshape(SEQUENCE_COUNT, blocks, block_rows, FACTOR_CHANNELS).transpose(
        1, 0, 2, 3
    )

    def forward_block(inputs):
        pair_rows, left_rows = inputs
        outer = (
            jnp.einsum("sic,sje->ijce", left_rows, right_side, preferred_element_type=jnp.float32)
            / SEQUENCE_COUNT
        )
        outer = outer.reshape(block_rows * cols_dev, FACTOR_CHANNELS * FACTOR_CHANNELS).astype(
            jnp.bfloat16
        )
        update = jnp.dot(outer, w_outer, preferred_element_type=jnp.float32)
        middle_state = (
            pair_rows.reshape(block_rows * cols_dev, channels).astype(jnp.float32) + update
        ).astype(jnp.bfloat16)
        xnorm = layer_normalize(middle_state.astype(jnp.float32))[0].astype(jnp.bfloat16)
        before = lax.optimization_barrier(
            jnp.dot(xnorm, w_expand, preferred_element_type=jnp.float32).astype(jnp.bfloat16)
        )
        hidden = jax.nn.silu(before.astype(jnp.float32)).astype(jnp.bfloat16)
        final = (
            middle_state.astype(jnp.float32)
            + jnp.dot(hidden, w_shrink, preferred_element_type=jnp.float32)
        ).astype(jnp.bfloat16)
        logits = jnp.dot(final, w_bins, preferred_element_type=jnp.float32).astype(jnp.bfloat16)
        return (middle_state, before, logits.reshape(block_rows, cols_dev * BINS))

    middle_state, before, logits = lax.map(forward_block, (pair_blocks, left_blocks))
    across = mirrored(logits.reshape(rows_dev, cols_dev * BINS), rows_dev, n_row, n_col).reshape(
        rows_dev, cols_dev, BINS
    )
    own = logits.reshape(rows_dev, cols_dev, BINS)
    scores = own.astype(jnp.float32) + across.astype(jnp.float32)
    scores = scores - jnp.max(scores, axis=-1, keepdims=True)
    expo = jnp.exp(scores)
    prob = expo / jnp.sum(expo, axis=-1, keepdims=True)
    onehot = (targets[:, :, None] == jnp.arange(BINS, dtype=jnp.int32)).astype(jnp.float32)
    row_mask = lax.dynamic_slice_in_dim(crop_mask, row_index * rows_dev, rows_dev).astype(
        jnp.float32
    )
    col_mask = lax.dynamic_slice_in_dim(crop_mask, col_index * cols_dev, cols_dev).astype(
        jnp.float32
    )
    weight = row_mask[:, None] * col_mask[None, :]
    dlogits = (2.0 * (prob - onehot) * weight[:, :, None]).astype(jnp.bfloat16)
    dlog_blocks = dlogits.reshape(blocks, block_rows * cols_dev, BINS)

    def backward_block(inputs):
        middle_row_block, before_rows, dlog_rows = inputs
        final_gradient = jnp.dot(dlog_rows, w_bins.T, preferred_element_type=jnp.float32)
        before_f = before_rows.astype(jnp.float32)
        sigma = jax.nn.sigmoid(before_f)
        slope = sigma * (1.0 + before_f * (1.0 - sigma))
        dhidden = (
            jnp.dot(
                final_gradient.astype(jnp.bfloat16), w_shrink.T, preferred_element_type=jnp.float32
            )
            * slope
        ).astype(jnp.bfloat16)
        normed_input_gradient = jnp.dot(dhidden, w_expand.T, preferred_element_type=jnp.float32)
        standardized_input, inverse_deviation = layer_normalize(
            middle_row_block.astype(jnp.float32)
        )
        middle_gradient = final_gradient + inverse_deviation * (
            normed_input_gradient
            - jnp.mean(normed_input_gradient, axis=-1, keepdims=True)
            - standardized_input
            * jnp.mean(normed_input_gradient * standardized_input, axis=-1, keepdims=True)
        )
        return middle_gradient.astype(jnp.bfloat16)

    grads = lax.map(backward_block, (middle_state, before, dlog_blocks))
    return grads.reshape(rows_dev, cols_dev, channels)


def solution(mesh):
    in_specs = (
        P("row", "col", None),
        P("row", "col", None),
        P("row", "col"),
        P(),
        P(),
        P(),
        P(),
        P(),
        P(),
    )
    out_specs = P("row", "col", None)
    return jax.shard_map(
        per_device, mesh=mesh, in_specs=in_specs, out_specs=out_specs, check_vma=False
    )
```

profile of v0, /device:TPU:1, one launch (start us, length us, event | category | flops | bytes accessed | tf_op | source)
XLA Modules:
  0.0 618.3 jit_solution(1737578397463702173)
XLA Ops:
  7.3 138.0 %all-gather.2.cloned.1.call-done = bf16[64,192,256]{2,1,0:T(8,128)(2,1)} async-done(((bf16[2,192,256]{2,1,0:T(8,128)(2,1)}), bf16[64,192,256]{2,1,0:T(8,128)(2,1)}) %all-gather.2.cloned.1.call-update) | async-done | bytes 6291472 | tf_op jit(solution)/shard_map/all_gather | solution.py:57
  145.3 5.2 convert_reduce_fusion.2
  150.5 4.4 fusion.54
  155.0 5.2 fusion.60
  164.0 62.7 %all-reduce.2.cloned.1.call-done = bf16[6,64,8,32]{1,3,2,0:T(8,128)(2,1)} async-done(((bf16[6,64,8,32]{1,3,2,0:T(8,128)(2,1)}), bf16[6,64,8,32]{1,3,2,0:T(8,128)(2,1)}) %all-reduce.2.cloned.1.call-update) | async-done | bytes 196624 | tf_op jit(solution)/shard_map/psum | solution.py:14
  226.7 158.3 %while.24 = (s32[]{:T(128)}, bf16[6,1536,128]{1,2,0:T(8,128)(2,1)}, bf16[6,1536,512]{2,1,0:T(8,128)(2,1)}, bf16[6,8,12288]{2,1,0:T(8,128)(2,1)}, bf16[6,8,192,12...) while((s32[]{:T(128)}, bf16[6,1536,128]{1,2,0:T(8,128)(2,1)}, ...), condition=%wide.region_6.7_spmd, body=%wide.region_3.6_spmd.sunk | while | flops 1043695104 | bytes 37036208 | solution.py:99
  226.7 2.5 fusion.107
  229.2 4.5 copy.80
  233.7 6.3 %convert_element_type.284 = bf16[1536,1024]{0,1:T(8,128)(2,1)S(1)} reshape(bf16[8,192,32,32]{1,0,3,2:T(8,128)(2,1)} %copy.80) | data formatting | bytes 6291456 | tf_op jit(solution)/shard_map/while/body/eval_jaxpr/convert_element_type | solution.py:80
  242.0 2.3 copy.79
  244.3 2.6 bitcast_dynamic-update-slice_fusion.4
  248.3 2.3 convolution_convert_fusion.5
  253.1 2.5 fusion.107
  255.6 4.5 copy.80
  260.1 6.3 %convert_element_type.284 = bf16[1536,1024]{0,1:T(8,128)(2,1)S(1)} reshape(bf16[8,192,32,32]{1,0,3,2:T(8,128)(2,1)} %copy.80) | data formatting | bytes 6291456 | tf_op jit(solution)/shard_map/while/body/eval_jaxpr/convert_element_type | solution.py:80
  268.4 2.3 copy.79
  270.7 2.6 bitcast_dynamic-update-slice_fusion.4
  274.6 2.3 convolution_convert_fusion.5
  279.5 2.5 fusion.107
  282.0 4.5 copy.80
  286.5 6.3 %convert_element_type.284 = bf16[1536,1024]{0,1:T(8,128)(2,1)S(1)} reshape(bf16[8,192,32,32]{1,0,3,2:T(8,128)(2,1)} %copy.80) | data formatting | bytes 6291456 | tf_op jit(solution)/shard_map/while/body/eval_jaxpr/convert_element_type | solution.py:80
  294.8 2.3 copy.79
  297.1 2.6 bitcast_dynamic-update-slice_fusion.4
  301.0 2.3 convolution_convert_fusion.5
  305.9 2.5 fusion.107
  308.3 4.5 copy.80
  312.8 6.3 %convert_element_type.284 = bf16[1536,1024]{0,1:T(8,128)(2,1)S(1)} reshape(bf16[8,192,32,32]{1,0,3,2:T(8,128)(2,1)} %copy.80) | data formatting | bytes 6291456 | tf_op jit(solution)/shard_map/while/body/eval_jaxpr/convert_element_type | solution.py:80
  321.1 2.3 copy.79
  323.4 2.6 bitcast_dynamic-update-slice_fusion.4
  327.3 2.3 convolution_convert_fusion.5
  332.2 2.5 fusion.107
  334.7 4.5 copy.80
  339.2 6.3 %convert_element_type.284 = bf16[1536,1024]{0,1:T(8,128)(2,1)S(1)} reshape(bf16[8,192,32,32]{1,0,3,2:T(8,128)(2,1)} %copy.80) | data formatting | bytes 6291456 | tf_op jit(solution)/shard_map/while/body/eval_jaxpr/convert_element_type | solution.py:80
  347.5 2.3 copy.79
  349.8 2.5 bitcast_dynamic-update-slice_fusion.4
  353.7 2.3 convolution_convert_fusion.5
  358.6 2.5 fusion.107
  361.1 4.5 copy.80
  365.6 6.3 %convert_element_type.284 = bf16[1536,1024]{0,1:T(8,128)(2,1)S(1)} reshape(bf16[8,192,32,32]{1,0,3,2:T(8,128)(2,1)} %copy.80) | data formatting | bytes 6291456 | tf_op jit(solution)/shard_map/while/body/eval_jaxpr/convert_element_type | solution.py:80
  373.9 2.3 copy.79
  376.1 2.6 bitcast_dynamic-update-slice_fusion.4
  380.1 2.3 convolution_convert_fusion.5
  385.0 2.0 reshape_reshape.7
  387.0 34.3 %all_to_all.26 = bf16[8,4,6,3072]{3,1,2,0:T(4,128)(2,1)S(1)} all-to-all(bf16[8,4,6,3072]{3,1,2,0:T(4,128)(2,1)S(1)} %bitcast.140), channel_id=1, replica_groups=mesh['row'=32,'col'=8] {'col'}, dimensions={0} | all-to-all | bytes 2359296 | tf_op jit(solution)/shard_map/all_to_all | solution.py:36
  421.7 50.7 %all_to_all.27 = bf16[32,1,6,3072]{3,2,1,0:T(8,128)(2,1)} all-to-all(bf16[32,1,6,3072]{3,2,1,0:T(8,128)(2,1)S(1)} %bitcast.139), channel_id=1, replica_groups=mesh['row'=32,'col'=8] {'row'}, dimensions={0} | all-to-all | bytes 2359296 | tf_op jit(solution)/shard_map/all_to_all | solution.py:39
  472.4 7.7 %all-to-all-start.2 = ((bf16[1,32,6,3072]{3,2,0,1:T(8,128)(2,1)}), bf16[1,32,6,3072]{3,2,0,1:T(8,128)(2,1)}, u32[]{:S(2)}, u32[]{:S(2)}) async-start(bf16[1,32,6,3072]{3,2,0,1:T(8,128)(2,1)} %bitcast.20), calls=%async_computation.2 | async-start | bytes 3145728 | tf_op jit(solution)/shard_map/all_to_all | solution.py:38
  482.1 3.6 reshape.139
  485.8 3.5 reshape.137
  489.3 27.8 %all-to-all-done.2 = bf16[1,32,6,3072]{3,2,0,1:T(8,128)(2,1)} async-done(((bf16[1,32,6,3072]{3,2,0,1:T(8,128)(2,1)}), bf16[1,32,6,3072]{3,2,0,1:T(8,128)(2,1)}, u32[]{:S(2)}, u32[]{:S(2)}) %all-to-all-start.2) | async-done | bytes 1179680 | tf_op jit(solution)/shard_map/all_to_all | solution.py:38
  517.1 2.1 copy_convert_fusion
  519.2 3.2 reshape.141
  522.4 3.0 copy.60
  526.1 2.4 fusion.63
  528.6 4.7 exponential_reduce_fusion
  533.3 7.9 %copy.59 = f32[48,4,8,6,64]{4,3,2,1,0:T(8,128)} copy(f32[48,4,8,6,64]{4,0,1,2,3:T(8,128)} %bitcast.138) | data formatting | bytes 4718592 | tf_op jit(solution)/shard_map/convert_element_type | solution.py:104
  541.3 6.6 %reshape.138 = f32[6,1536,64]{2,1,0:T(8,128)} reshape(f32[48,4,8,6,64]{4,3,2,1,0:T(8,128)} %copy.59) | data formatting | bytes 4718592 | tf_op jit(solution)/shard_map/convert_element_type | solution.py:104
  547.9 8.4 %multiply_convert_fusion.1 = bf16[6,1536,64]{2,1,0:T(8,128)(2,1)} fusion(f32[6,1536,64]{2,1,0:T(8,128)} %reshape.137, f32[6,1536,64]{2,1,0:T(8,128)} %reshape.138, f32[6,1536]{1,0:T(8,128)S(1)} %multiply_multiply_fusion, s32[6,1536]{1,0:T(8,128)S(1)} %eq.22, f32[6,1536]{1,0:T(8,128)S(1)} %div.58, f32[6,1536]{1,0:T(8,128)S(1)} %sub.64), kind=kLoop, calls=%fused_computation.82 | loop fusion | flops 4718592 | bytes 6045696 | tf_op jit(solution)/shard_map/convert_element_type | solution.py:116
  556.3 54.4 %while.25 = (s32[]{:T(128)}, bf16[6,1536,128]{2,1,0:T(8,128)(2,1)}, bf16[6,1536,64]{2,1,0:T(8,128)(2,1)}, bf16[128,64]{0,1:T(8,128)(2,1)S(1)}, bf16[6,1536,128]{...) while((s32[]{:T(128)}, bf16[6,1536,128]{2,1,0:T(8,128)(2,1)}, ...), condition=%wide.region_14.15_spmd, body=%wide.region_9.14_spmd.sunk | while | flops 440010240 | bytes 12193377 | solution.py:143
  559.8 2.9 fusion.115
  568.8 3.0 fusion.115
  577.8 2.9 fusion.115
  586.8 3.0 fusion.115
  595.8 2.9 fusion.115
  604.8 3.0 fusion.115
  (205 shorter events, 79.7 us)
Async XLA Ops:
  6.5 148.5 %copy-start = (bf16[256,64]{0,1:T(8,128)(2,1)S(1)}, bf16[256,64]{0,1:T(8,128)(2,1)}, u32[]{:S(2)}) copy-start(bf16[256,64]{0,1:T(8,128)(2,1)} %param.17) | copy-start | bytes 98308
  6.5 138.8 %all-gather.2.cloned.1.call-start = ((), (), s32[]{:S(2)}) async-start(), calls=%async_computation.3 | async-start | bytes 6488064 | tf_op jit(solution)/shard_map/all_gather | solution.py:57
  7.3 219.5 %all-reduce.2.cloned.1.call-start = ((), (), s32[]{:S(2)}) async-start(), calls=%async_computation.4 | async-start | bytes 786432 | tf_op jit(solution)/shard_map/psum | solution.py:14
  145.3 5.2 copy-start.3
  160.4 66.3 %copy-start.5 = (bf16[1024,128]{1,0:T(8,128)(2,1)S(1)}, bf16[1024,128]{1,0:T(8,128)(2,1)}, u32[]{:S(2)}) copy-start(bf16[1024,128]{1,0:T(8,128)(2,1)} %param.18) | copy-start | bytes 786436
  160.4 66.3 %copy-start.8 = (bf16[128,64]{0,1:T(8,128)(2,1)S(1)}, bf16[128,64]{0,1:T(8,128)(2,1)}, u32[]{:S(2)}) copy-start(bf16[128,64]{0,1:T(8,128)(2,1)} %param.21) | copy-start | bytes 49156
  244.3 3.3 copy-start.6
  246.9 0.7 copy-start.2
  270.7 3.3 copy-start.6
  273.3 0.7 copy-start.2
  297.1 3.3 copy-start.6
  299.6 0.7 copy-start.2
  323.4 3.3 copy-start.6
  326.0 0.7 copy-start.2
  349.8 3.3 copy-start.6
  352.4 0.7 copy-start.2
  376.1 3.3 copy-start.6
  378.7 0.7 copy-start.2
  421.7 60.3 %copy-start.9 = (s32[48,192]{1,0:T(8,128)S(1)}, s32[48,192]{1,0:T(8,128)}, u32[]{:S(2)}) copy-start(s32[48,192]{1,0:T(8,128)} %param.15) | copy-start | bytes 110596
  421.7 60.4 %copy-start.4 = (bf16[6,8,12288]{2,1,0:T(8,128)(2,1)S(1)}, bf16[6,8,12288]{2,1,0:T(8,128)(2,1)}, u32[]{:S(2)}) copy-start(bf16[6,8,12288]{2,1,0:T(8,128)(2,1)} %get-tuple-element.106) | copy-start | bytes 3538948
  472.4 44.7 %all-to-all-start.2 = ((bf16[1,32,6,3072]{3,2,0,1:T(8,128)(2,1)}), bf16[1,32,6,3072]{3,2,0,1:T(8,128)(2,1)}, u32[]{:S(2)}, u32[]{:S(2)}) async-start(bf16[1,32,6,3072]{3,2,0,1:T(8,128)(2,1)} %bitcast.20), calls=%async_computation.2 | async-start | bytes 3145728 | tf_op jit(solution)/shard_map/all_to_all | solution.py:38
  522.4 3.6 slice-start
  522.4 3.7 slice-start.1
  547.9 8.4 %copy-start.7 = (bf16[128,512]{1,0:T(8,128)(2,1)S(1)}, bf16[128,512]{1,0:T(8,128)(2,1)}, u32[]{:S(2)}) copy-start(bf16[128,512]{1,0:T(8,128)(2,1)} %get-tuple-element.426) | copy-start | bytes 393220
  547.9 8.4 %copy-start.10 = (bf16[512,128]{1,0:T(8,128)(2,1)S(1)}, bf16[512,128]{1,0:T(8,128)(2,1)}, u32[]{:S(2)}) copy-start(bf16[512,128]{1,0:T(8,128)(2,1)} %get-tuple-element.433) | copy-start | bytes 393220
  610.7 0.8 copy-start.1
Sparse Core Ops, SparseCore 0:
  10.8 134.4 all-gather.1
  162.5 64.1 all-reduce.1
where the time goes:
time: 621 us; the launch traced here: 618 us
  waiting for transfers between devices  229 us (37%)
  local copies, waits for them, and re-layouts  148 us (24%)
  blocking collectives  85 us (14%)
  matrix products  78 us (13%)
  other arithmetic  55.8 us (9%)
  between operations  13.7 us (2%)
  starting transfers between devices  7.75 us (1%)
    all_gather x1, waiting for transfers between devices, per_device(): lax.all_gather(alignment, 'row', axis=0, tiled=True)  138 us
    convert_element_type x12, local copies, waits for them, and re-layouts, forward_block(): outer.reshape(block_rows * cols_dev, FACTOR_CHANNELS * FACTOR_CHANNELS)  64.8 us
    psum x1, waiting for transfers between devices, from_root(): return lax.psum(jnp.where(mine, shard, jnp.zeros_like(shard)), axis)  62.7 us
    all_to_all x1, blocking collectives, mirrored(): lax.all_to_all(regrouped, 'row', split_axis=0, concat_axis=1, tiled=True)  50.7 us
    all_to_all x1, blocking collectives, mirrored(): lax.all_to_all(sectioned, 'col', split_axis=0, concat_axis=0, tiled=True)  34.3 us
    convert_element_type x6, local copies, waits for them, and re-layouts, per_device(): scores = own.astype(jnp.float32) + across.astype(jnp.float32)  27.8 us
    all_to_all x1, waiting for transfers between devices, mirrored(): lax.all_to_all(lax.all_to_all(regrouped, 'row', split_axis=0, concat_axis...  27.8 us
    dot_general x6, matrix products, backward_block(): jnp.dot(dhidden, w_expand.T, preferred_element_type=jnp.float32)  17.7 us
  transfers between devices with their start and end apart: 3, of which 3 were waited for; matrix products, arithmetic and copies ran while one was open for 2% of the time, Pallas kernels for 0%

commit v1 on v0

--- a/solution.py
+++ b/solution.py
@@ -7,6 +7,11 @@
 BINS = 64
 SEQUENCE_COUNT = 64
 epsilon = 1e-05
+
+
+def gather_over(x, mesh_axis, along):
+    sent = jnp.stack([x] * lax.axis_size(mesh_axis))
+    return jnp.concatenate(lax.all_to_all(sent, mesh_axis, 0, 0), axis=along)
 
 
 def from_root(shard, axis, root):
@@ -54,7 +59,7 @@
     ratio = n_row // n_col
     row_index = lax.axis_index("row")
     col_index = lax.axis_index("col")
-    factors = norm_project(lax.all_gather(alignment, "row", axis=0, tiled=True), projection_weight)
+    factors = norm_project(gather_over(alignment, "row", 0), projection_weight)
     factors = factors.reshape(SEQUENCE_COUNT, cols_dev, 2 * FACTOR_CHANNELS)
     right_side = factors[:, :, FACTOR_CHANNELS:]
     own_left = lax.dynamic_slice_in_dim(

time: 621 us -> 669 us (1.077)
  waiting for transfers between devices: 229 us -> 252 us
  starting transfers between devices: 7.75 us -> 22.3 us
  other arithmetic: 55.8 us -> 64.5 us
    all_gather x1 -> x0, waiting for transfers between devices: 138 us -> none  [per_device(): lax.all_gather(alignment, 'row', axis=0, tiled=True)]
    all_to_all x0 -> x1, waiting for transfers between devices: none -> 137 us  [gather_over(): return jnp.concatenate(lax.all_to_all(sent, mesh_axis, 0, 0), axis=along)]
    psum x1, waiting for transfers between devices: 62.7 us -> 87.1 us  [from_root(): return lax.psum(jnp.where(mine, shard, jnp.zeros_like(shard)), axis)]
    all_to_all x0 -> x1, starting transfers between devices: none -> 14.6 us  [gather_over(): return jnp.concatenate(lax.all_to_all(sent, mesh_axis, 0, 0), axis=along)]
    convert_element_type x0 -> x1, other arithmetic: none -> 7.13 us  [norm_project(): layer_normalize(shard_rows.astype(jnp.float32))[0].astype(jnp.bfloat16)]
where the time goes in v1:
time: 669 us; the launch traced here: 666 us
  waiting for transfers between devices  252 us (38%)
  local copies, waits for them, and re-layouts  152 us (23%)
  blocking collectives  85 us (13%)
  matrix products  74.9 us (11%)
  other arithmetic  64.5 us (10%)
  starting transfers between devices  22.3 us (3%)
  between operations  13.7 us (2%)
    all_to_all x1, waiting for transfers between devices, gather_over(): return jnp.concatenate(lax.all_to_all(sent, mesh_axis, 0, 0), axis=along)  137 us
    psum x1, waiting for transfers between devices, from_root(): return lax.psum(jnp.where(mine, shard, jnp.zeros_like(shard)), axis)  87.1 us
    convert_element_type x12, local copies, waits for them, and re-layouts, forward_block(): outer.reshape(block_rows * cols_dev, FACTOR_CHANNELS * FACTOR_CHANNELS)  64.8 us
    all_to_all x1, blocking collectives, mirrored(): lax.all_to_all(regrouped, 'row', split_axis=0, concat_axis=1, tiled=True)  50.7 us
    all_to_all x1, blocking collectives, mirrored(): lax.all_to_all(sectioned, 'col', split_axis=0, concat_axis=0, tiled=True)  34.3 us
    convert_element_type x6, local copies, waits for them, and re-layouts, per_device(): scores = own.astype(jnp.float32) + across.astype(jnp.float32)  27.8 us
    all_to_all x1, waiting for transfers between devices, mirrored(): lax.all_to_all(lax.all_to_all(regrouped, 'row', split_axis=0, concat_axis...  27.8 us
    dot_general x6, matrix products, backward_block(): jnp.dot(dhidden, w_expand.T, preferred_element_type=jnp.float32)  17.7 us
  transfers between devices with their start and end apart: 3, of which 3 were waited for; matrix products, arithmetic and copies ran while one was open for 2% of the time, Pallas kernels for 0%

profile of v1, /device:TPU:1, one launch (start us, length us, event | category | flops | bytes accessed | tf_op | source)
XLA Modules:
  0.0 665.9 jit_solution(2175141602042465207)
XLA Ops:
  6.5 4.3 stack.2
  10.9 14.6 %all-to-all-start = ((bf16[32,2,192,256]{3,2,1,0:T(8,128)(2,1)}), bf16[32,2,192,256]{3,2,1,0:T(8,128)(2,1)}, u32[]{:S(2)}, u32[]{:S(2)}) async-start(bf16[32,2,192,256]{3,2,1,0:T(8,128)(2,1)} %stack.2), calls=%async_computation | async-start | bytes 12582912 | tf_op jit(solution)/shard_map/all_to_all | solution.py:14
  25.6 137.2 %all-to-all-done = bf16[32,2,192,256]{3,2,1,0:T(8,128)(2,1)} async-done(((bf16[32,2,192,256]{3,2,1,0:T(8,128)(2,1)}), bf16[32,2,192,256]{3,2,1,0:T(8,128)(2,1)}, u32[]{:S(2)}, u32[]{:S(2)}) %all-to-all-start) | async-done | bytes 6291488 | tf_op jit(solution)/shard_map/all_to_all | solution.py:14
  162.8 5.1 convert_reduce_fusion.2
  168.0 6.1 multiply_reduce_fusion
  174.2 7.1 %fusion.53 = bf16[64,192,256]{2,1,0:T(8,128)(2,1)S(1)} fusion(bf16[32,2,192,256]{3,2,1,0:T(8,128)(2,1)} %all-to-all-done, f32[64,192]{1,0:T(8,128)S(1)} %rsqrt.28, f32[64,192]{1,0:T(8,128)S(1)} %div.59), kind=kLoop, calls=%fused_computation.74 | loop fusion | flops 12582912 | bytes 12681216 | tf_op jit(solution)/shard_map/convert_element_type | solution.py:30
  187.3 87.1 %all-reduce.2.cloned.1.call-done = bf16[6,64,8,32]{1,3,2,0:T(8,128)(2,1)} async-done(((bf16[6,64,8,32]{1,3,2,0:T(8,128)(2,1)}), bf16[6,64,8,32]{1,3,2,0:T(8,128)(2,1)}) %all-reduce.2.cloned.1.call-update) | async-done | bytes 196624 | tf_op jit(solution)/shard_map/psum | solution.py:19
  274.3 158.3 %while.24 = (s32[]{:T(128)}, bf16[6,1536,128]{1,2,0:T(8,128)(2,1)}, bf16[6,1536,512]{2,1,0:T(8,128)(2,1)}, bf16[6,8,12288]{2,1,0:T(8,128)(2,1)}, bf16[6,8,192,12...) while((s32[]{:T(128)}, bf16[6,1536,128]{1,2,0:T(8,128)(2,1)}, ...), condition=%wide.region_6.7_spmd, body=%wide.region_3.6_spmd.sunk | while | flops 1043695104 | bytes 37036208 | solution.py:104
  274.3 2.5 fusion.99
  276.8 4.5 copy.80
  281.3 6.3 convert_element_type.281
  289.6 2.3 copy.79
  291.9 2.6 bitcast_dynamic-update-slice_fusion.4
  295.9 2.3 convolution_convert_fusion.6
  300.7 2.5 fusion.99
  303.2 4.5 copy.80
  307.7 6.3 convert_element_type.281
  316.0 2.3 copy.79
  318.3 2.6 bitcast_dynamic-update-slice_fusion.4
  322.2 2.3 convolution_convert_fusion.6
  327.1 2.5 fusion.99
  329.6 4.5 copy.80
  334.1 6.3 convert_element_type.281
  342.4 2.3 copy.79
  344.7 2.6 bitcast_dynamic-update-slice_fusion.4
  348.6 2.3 convolution_convert_fusion.6
  353.5 2.5 fusion.99
  356.0 4.5 copy.80
  360.4 6.3 convert_element_type.281
  368.7 2.3 copy.79
  371.0 2.6 bitcast_dynamic-update-slice_fusion.4
  374.9 2.3 convolution_convert_fusion.6
  379.8 2.5 fusion.99
  382.3 4.5 copy.80
  386.8 6.3 convert_element_type.281
  395.1 2.3 copy.79
  397.4 2.5 bitcast_dynamic-update-slice_fusion.4
  401.3 2.3 convolution_convert_fusion.6
  406.2 2.5 fusion.99
  408.7 4.5 copy.80
  413.2 6.3 convert_element_type.281
  421.5 2.3 copy.79
  423.8 2.6 bitcast_dynamic-update-slice_fusion.4
  427.7 2.3 convolution_convert_fusion.6
  434.6 34.3 %all_to_all.31 = bf16[8,4,6,3072]{3,1,2,0:T(4,128)(2,1)S(1)} all-to-all(bf16[8,4,6,3072]{3,1,2,0:T(4,128)(2,1)S(1)} %bitcast.147), channel_id=1, replica_groups=mesh['row'=32,'col'=8] {'col'}, dimensions={0} | all-to-all | bytes 2359296 | tf_op jit(solution)/shard_map/all_to_all | solution.py:41
  469.3 50.7 %all_to_all.32 = bf16[32,1,6,3072]{3,2,1,0:T(8,128)(2,1)} all-to-all(bf16[32,1,6,3072]{3,2,1,0:T(8,128)(2,1)S(1)} %bitcast.146), channel_id=1, replica_groups=mesh['row'=32,'col'=8] {'row'}, dimensions={0} | all-to-all | bytes 2359296 | tf_op jit(solution)/shard_map/all_to_all | solution.py:44
  520.1 7.7 %all-to-all-start.3 = ((bf16[1,32,6,3072]{3,2,0,1:T(8,128)(2,1)}), bf16[1,32,6,3072]{3,2,0,1:T(8,128)(2,1)}, u32[]{:S(2)}, u32[]{:S(2)}) async-start(bf16[1,32,6,3072]{3,2,0,1:T(8,128)(2,1)} %bitcast.21), calls=%async_computation.3 | async-start | bytes 3145728 | tf_op jit(solution)/shard_map/all_to_all | solution.py:43
  529.8 3.6 reshape.162
  533.4 3.5 reshape.160
  536.9 27.8 %all-to-all-done.3 = bf16[1,32,6,3072]{3,2,0,1:T(8,128)(2,1)} async-done(((bf16[1,32,6,3072]{3,2,0,1:T(8,128)(2,1)}), bf16[1,32,6,3072]{3,2,0,1:T(8,128)(2,1)}, u32[]{:S(2)}, u32[]{:S(2)}) %all-to-all-start.3) | async-done | bytes 1179680 | tf_op jit(solution)/shard_map/all_to_all | solution.py:43
  566.8 3.2 reshape.164
  570.0 3.0 copy.60
  573.7 2.4 fusion.54
  576.2 4.7 exponential_reduce_fusion
  580.9 7.9 %copy.59 = f32[48,4,8,6,64]{4,3,2,1,0:T(8,128)} copy(f32[48,4,8,6,64]{4,0,1,2,3:T(8,128)} %bitcast.145) | data formatting | bytes 4718592 | tf_op jit(solution)/shard_map/convert_element_type | solution.py:109
  588.9 6.6 reshape.161
  595.5 8.4 %multiply_convert_fusion.1 = bf16[6,1536,64]{2,1,0:T(8,128)(2,1)} fusion(f32[6,1536,64]{2,1,0:T(8,128)} %reshape.160, f32[6,1536,64]{2,1,0:T(8,128)} %reshape.161, f32[6,1536]{1,0:T(8,128)S(1)} %multiply_multiply_fusion, s32[6,1536]{1,0:T(8,128)S(1)} %eq.22, f32[6,1536]{1,0:T(8,128)S(1)} %div.61, f32[6,1536]{1,0:T(8,128)S(1)} %sub.71), kind=kLoop, calls=%fused_computation.78 | loop fusion | flops 4718592 | bytes 6045696 | tf_op jit(solution)/shard_map/convert_element_type | solution.py:121
  603.9 54.4 %while.25 = (s32[]{:T(128)}, bf16[6,1536,128]{2,1,0:T(8,128)(2,1)}, bf16[6,1536,64]{2,1,0:T(8,128)(2,1)}, bf16[128,64]{0,1:T(8,128)(2,1)S(1)}, bf16[6,1536,128]{...) while((s32[]{:T(128)}, bf16[6,1536,128]{2,1,0:T(8,128)(2,1)}, ...), condition=%wide.region_14.15_spmd, body=%wide.region_9.14_spmd.sunk | while | flops 440010240 | bytes 12193377 | solution.py:148
  607.4 2.9 fusion.107
  616.4 3.0 fusion.107
  625.4 2.9 fusion.107
  634.4 3.0 fusion.107
  643.4 2.9 fusion.107
  652.5 3.0 fusion.107
  (206 shorter events, 85.3 us)
Async XLA Ops:
  6.5 174.8 %copy-start = (bf16[256,64]{0,1:T(8,128)(2,1)S(1)}, bf16[256,64]{0,1:T(8,128)(2,1)}, u32[]{:S(2)}) copy-start(bf16[256,64]{0,1:T(8,128)(2,1)} %param.17) | copy-start | bytes 98308
  10.9 151.9 %all-to-all-start = ((bf16[32,2,192,256]{3,2,1,0:T(8,128)(2,1)}), bf16[32,2,192,256]{3,2,1,0:T(8,128)(2,1)}, u32[]{:S(2)}, u32[]{:S(2)}) async-start(bf16[32,2,192,256]{3,2,1,0:T(8,128)(2,1)} %stack.2), calls=%async_computation | async-start | bytes 12582912 | tf_op jit(solution)/shard_map/all_to_all | solution.py:14
  25.5 248.8 %all-reduce.2.cloned.1.call-start = ((), (), s32[]{:S(2)}) async-start(), calls=%async_computation.4 | async-start | bytes 786432 | tf_op jit(solution)/shard_map/psum | solution.py:19
  183.7 90.6 %copy-start.4 = (bf16[1024,128]{1,0:T(8,128)(2,1)S(1)}, bf16[1024,128]{1,0:T(8,128)(2,1)}, u32[]{:S(2)}) copy-start(bf16[1024,128]{1,0:T(8,128)(2,1)} %param.18) | copy-start | bytes 786436
  183.7 90.6 %copy-start.7 = (bf16[128,64]{0,1:T(8,128)(2,1)S(1)}, bf16[128,64]{0,1:T(8,128)(2,1)}, u32[]{:S(2)}) copy-start(bf16[128,64]{0,1:T(8,128)(2,1)} %param.21) | copy-start | bytes 49156
  291.9 3.3 copy-start.5
  294.5 0.7 copy-start.2
  318.3 3.3 copy-start.5
  320.9 0.7 copy-start.2
  344.7 3.3 copy-start.5
  347.3 0.7 copy-start.2
  371.0 3.3 copy-start.5
  373.6 0.7 copy-start.2
  397.4 3.3 copy-start.5
  400.0 0.7 copy-start.2
  423.8 3.3 copy-start.5
  426.3 0.7 copy-start.2
  469.3 60.3 %copy-start.8 = (s32[48,192]{1,0:T(8,128)S(1)}, s32[48,192]{1,0:T(8,128)}, u32[]{:S(2)}) copy-start(s32[48,192]{1,0:T(8,128)} %param.15) | copy-start | bytes 110596
  469.3 60.4 %copy-start.3 = (bf16[6,8,12288]{2,1,0:T(8,128)(2,1)S(1)}, bf16[6,8,12288]{2,1,0:T(8,128)(2,1)}, u32[]{:S(2)}) copy-start(bf16[6,8,12288]{2,1,0:T(8,128)(2,1)} %get-tuple-element.106) | copy-start | bytes 3538948
  520.1 44.7 %all-to-all-start.3 = ((bf16[1,32,6,3072]{3,2,0,1:T(8,128)(2,1)}), bf16[1,32,6,3072]{3,2,0,1:T(8,128)(2,1)}, u32[]{:S(2)}, u32[]{:S(2)}) async-start(bf16[1,32,6,3072]{3,2,0,1:T(8,128)(2,1)} %bitcast.21), calls=%async_computation.3 | async-start | bytes 3145728 | tf_op jit(solution)/shard_map/all_to_all | solution.py:43
  570.0 3.6 slice-start
  570.0 3.7 slice-start.1
  595.5 8.4 %copy-start.6 = (bf16[128,512]{1,0:T(8,128)(2,1)S(1)}, bf16[128,512]{1,0:T(8,128)(2,1)}, u32[]{:S(2)}) copy-start(bf16[128,512]{1,0:T(8,128)(2,1)} %get-tuple-element.426) | copy-start | bytes 393220
  595.5 8.4 %copy-start.9 = (bf16[512,128]{1,0:T(8,128)(2,1)S(1)}, bf16[512,128]{1,0:T(8,128)(2,1)}, u32[]{:S(2)}) copy-start(bf16[512,128]{1,0:T(8,128)(2,1)} %get-tuple-element.431) | copy-start | bytes 393220
  658.3 0.8 copy-start.1
Sparse Core Ops, SparseCore 0:
  185.8 88.4 all-reduce.1
